TPU v7x, 768 devices: a whole 4x8x12 slice. The times are simulated.
768 devices in a mesh: ctx: 192 (over z, y_lo, x), head: 4 (over y_hi, core).
Axes of the slice: x: 4, y: 8 (y_hi: 2, y_lo: 4; y = y_hi * 4 + y_lo), z: 12, core: 2. Of those that a mesh axis runs over, the one named last changes fastest.
Arguments:
- hidden: bfloat16 [98304, 4096], P('ctx'), may hold values from -20 to 20
- w_query: bfloat16 [4096, 2048], P(None, 'head'), may hold values from -2 to 2
- key_projection: bfloat16 [4096, 512], P(None, 'head'), may hold values from -2 to 2
- value_projection: bfloat16 [4096, 512], P(None, 'head'), may hold values from -0.09375 to 0.09375
- q_gain: float32 [128], replicated, may hold values from 0.5 to 5
- key_norm_gain: float32 [128], replicated, may hold values from 0.5 to 5
- starts: int32 [384], replicated, may hold values from 0 to 98048, as said below
Outputs:
- attended: bfloat16 [98304, 2048], P(('ctx', 'head'))
Inputs may be any that keep to these rules, and one draw needn't show every extreme that they name: starts is 256 times a permutation of 0 to 383.
All inputs are finite; a program needn't handle non-finite values.
Results may differ from a plain program's by a relative error of at most 0.0085.
The roundings to bfloat16 on the way count: a program that leaves them out, or rounds other values in their place, can miss the bound.
Values may be sent and summed in bfloat16 or wider, within the bound.
A program may use at most 32 MiB of HBM per device.

v0:
```python
import jax
import jax.numpy as jnp
from jax import lax
from jax.sharding import PartitionSpec as P


def from_behind(block, axis, distance):
    devices = range(lax.axis_size(axis))
    route = [((i - distance) % len(devices), i) for i in devices]
    return lax.ppermute(block, axis, route)


def rms_scaled(rows, weight):
    return rows * lax.rsqrt(jnp.mean(rows * rows, axis=-1, keepdims=True) + 1e-06) * weight


def rotated(rows, positions):
    width = rows.shape[-1] // 2
    freqs = jnp.power(
        jnp.float32(1000000.0), -jnp.arange(width, dtype=jnp.float32) * 2.0 / (2 * width)
    )
    angles = positions.astype(jnp.float32)[:, None] * freqs[None, :]
    cosine = jnp.cos(angles)[:, None, :]
    sine = jnp.sin(angles)[:, None, :]
    first = rows[..., :width]
    second = rows[..., width:]
    return jnp.concatenate(
        [first * cosine - second * sine, second * cosine + first * sine], axis=-1
    )


def projected_rows(hidden, weight, gain, positions, heads):
    rows = jnp.dot(hidden, weight, preferred_element_type=jnp.float32)
    rows = rows.reshape(hidden.shape[0], heads, -1)
    return rotated(rms_scaled(rows, gain), positions).astype(jnp.bfloat16)


def block_positions(starts, index, half_len):
    pair = lax.dynamic_slice(starts, (2 * index,), (2,))
    offsets = jnp.arange(2 * half_len, dtype=jnp.int32)
    return jnp.where(offsets < half_len, pair[0] + offsets, pair[1] + offsets - half_len)


def attend(queries, key_rows, value_rows, q_pos, k_pos):
    count, q_heads, head_dim = queries.shape
    kv_heads = key_rows.shape[1]
    group_size = q_heads // kv_heads
    grouped = queries.reshape(count, kv_heads, group_size, head_dim)
    visible = k_pos[None, :] <= q_pos[:, None]

    def one_member(member):
        scores = jnp.einsum(
            "qkd,skd->kqs", member, key_rows, preferred_element_type=jnp.float32
        ) * head_dim ** (-0.5)
        scores = jnp.where(visible[None], scores, -1e30)
        top = jnp.max(scores, axis=-1, keepdims=True)
        weights = jnp.exp(scores - top)
        weights = (weights / jnp.sum(weights, axis=-1, keepdims=True)).astype(jnp.bfloat16)
        return jnp.einsum(
            "kqs,skd->qkd", weights, value_rows, preferred_element_type=jnp.float32
        ).astype(jnp.bfloat16)

    members = jnp.moveaxis(grouped, 2, 0)
    outputs = lax.map(one_member, members)
    return jnp.moveaxis(outputs, 0, 2).reshape(count, q_heads * head_dim)


def shards(hidden, w_query, key_projection, value_projection, q_gain, key_norm_gain, starts):
    block_len = hidden.shape[0]
    half_len = block_len // 2
    head_dim = q_gain.shape[0]
    q_heads = w_query.shape[1] // head_dim
    kv_heads = key_projection.shape[1] // head_dim
    ctx_count = lax.axis_size("ctx")
    ctx_index = lax.axis_index("ctx")
    own_pos = block_positions(starts, ctx_index, half_len)
    near_pos = block_positions(starts, (ctx_index + ctx_count - 1) % ctx_count, half_len)
    far_pos = block_positions(starts, (ctx_index + ctx_count - 2) % ctx_count, half_len)
    queries = projected_rows(hidden, w_query, q_gain, own_pos, q_heads)
    rotated_keys = projected_rows(hidden, key_projection, key_norm_gain, own_pos, kv_heads)
    value_rows = jnp.dot(hidden, value_projection, preferred_element_type=jnp.float32).astype(
        jnp.bfloat16
    )
    value_rows = value_rows.reshape(block_len, kv_heads, head_dim)
    near_keys, near_vals = from_behind((rotated_keys, value_rows), "ctx", 1)
    far_keys, far_vals = from_behind((near_keys, near_vals), "ctx", 1)
    key_all = jnp.concatenate([rotated_keys, near_keys, far_keys], axis=0)
    val_all = jnp.concatenate([value_rows, near_vals, far_vals], axis=0)
    pos_all = jnp.concatenate([own_pos, near_pos, far_pos], axis=0)
    attended = attend(queries, key_all, val_all, own_pos, pos_all)
    return lax.all_to_all(attended, "head", split_axis=0, concat_axis=1, tiled=True)


def solution(mesh):
    return jax.shard_map(
        shards,
        mesh=mesh,
        in_specs=(P("ctx", None), P(None, "head"), P(None, "head"), P(None, "head"), P(), P(), P()),
        out_specs=P(("ctx", "head"), None),
        check_vma=False,
    )
```

profile of v0, /device:TPU:1, one launch (start us, length us, event | category | flops | bytes accessed | tf_op | source)
XLA Modules:
  0.0 75.3 jit_solution(13753299235726174607)
XLA Ops:
  0.0 0.0 copy-start
  0.0 0.9 %fusion.26 = (s32[2]{0:T(128)S(1)}, s32[2]{0:T(128)S(1)}, s32[2]{0:T(128)S(1)}) fusion(s32[384]{0:T(512)} %param.15, s32[]{:T(128)S(6)} %select_n.45, s32[]{:T(128)S(6)} %select_n.42, s32[]{:T(128)S(6)} %select_n.48), kind=kLoop, calls=%fused_computation.51 | loop fusion | bytes 60 | tf_op jit(solution)/shard_map/dynamic_slice | solution.py:39
  0.9 0.6 fusion.29
  1.5 0.0 copy-done
  1.6 3.9 %multiply_reduce_fusion.1 = (f32[512]{0:T(512)S(1)}, f32[512,128]{0,1:T(8,128)S(1)}) fusion(bf16[512,4096]{1,0:T(8,128)(2,1)} %param.9, bf16[4096,128]{1,0:T(8,128)(2,1)S(1)} %copy-done), kind=kOutput, calls=%fused_computation.27 | convolution fusion | flops 537001472 | bytes 5507072 | tf_op jit(solution)/shard_map/dot_general | solution.py:33
  5.4 1.3 %fusion.24 = f32[512]{0:T(512)S(1)} fusion(s32[]{:T(128)} %bitcast.2, s32[]{:T(128)} %bitcast.1), kind=kLoop, calls=%fused_computation.49 | loop fusion | flops 3072 | bytes 2056 | tf_op jit(solution)/shard_map/convert_element_type | solution.py:22
  6.8 0.1 multiply_bitcast_fusion
  6.9 0.0 copy-start.4
  6.9 0.6 fusion.21
  7.5 4.1 %collective-permute-start = (bf16[512,1,128]{0,2,1:T(8,128)(2,1)S(1)}, bf16[512,1,128]{0,2,1:T(8,128)(2,1)S(1)}, u32[]{:S(2)}, u32[]{:S(2)}) collective-permute-start(bf16[512,1,128]{0,2,1:T(8,128)(2,1)S(1)} %pad_maximum_fusion.2), channel_id=1, source_target_pairs={{764,0},{0,4},{4,8},{8,12},{12,16},{16,20},{20,24},{24,28},{28,32}... | collective-permute-start | bytes 393224 | tf_op jit(solution)/shard_map/ppermute | solution.py:10
  11.5 1.3 %fusion.13 = bf16[512,1,128]{2,0,1:T(8,128)(2,1)S(1)} fusion(bf16[512,4096]{1,0:T(8,128)(2,1)S(1)} %copy-done.1, bf16[4096,128]{1,0:T(8,128)(2,1)S(1)} %copy-done.5), kind=kOutput, calls=%fused_computation.16 | convolution fusion | flops 536936448 | bytes 5373952 | tf_op jit(solution)/shard_map/dot_general | solution.py:81
  12.8 3.1 %collective-permute-start.2 = (bf16[512,1,128]{2,0,1:T(8,128)(2,1)S(1)}, bf16[512,1,128]{2,0,1:T(8,128)(2,1)S(1)}, u32[]{:S(2)}, u32[]{:S(2)}) collective-permute-start(bf16[512,1,128]{2,0,1:T(8,128)(2,1)S(1)} %fusion.13), channel_id=1, source_target_pairs={{764,0},{0,4},{4,8},{8,12},{12,16},{16,20},{20,24},{24,28},{28,32}... | collective-permute-start | bytes 393224 | tf_op jit(solution)/shard_map/ppermute | solution.py:10
  15.9 0.5 multiply_cosine_fusion.1
  16.5 1.3 %add_select_fusion.2 = s32[512]{0:T(512)S(1)} fusion(s32[]{:T(128)} %bitcast.2, s32[]{:T(128)} %bitcast.1), kind=kLoop, calls=%fused_computation.46 | loop fusion | flops 2560 | bytes 2056 | tf_op jit(solution)/shard_map/jit(_where)/select_n | solution.py:41
  17.8 0.0 copy-done.4
  17.8 0.0 copy-start.3
  17.8 2.4 %multiply_reduce_fusion = (f32[512,4]{0,1:T(4,128)S(1)}, f32[512,512]{0,1:T(8,128)S(1)}) fusion(bf16[512,4096]{1,0:T(8,128)(2,1)S(1)} %copy-done.1, bf16[4096,512]{1,0:T(8,128)(2,1)S(1)} %copy-done.4), kind=kOutput, calls=%fused_computation.18 | convolution fusion | flops 2148005888 | bytes 9445376 | tf_op jit(solution)/shard_map/dot_general | solution.py:33
  20.2 0.6 fusion.27
  20.9 0.0 copy-done.3
  20.9 0.2 multiply_multiply_fusion
  21.1 0.2 fusion.14
  21.2 1.3 %add_select_fusion = s32[512]{0:T(512)S(1)} fusion(s32[]{:T(128)} %bitcast.11, s32[]{:T(128)} %bitcast.10), kind=kLoop, calls=%fused_computation.43 | loop fusion | flops 2560 | bytes 2056 | tf_op jit(solution)/shard_map/jit(_where)/select_n | solution.py:41
  22.5 1.3 %add_select_fusion.1 = s32[512]{0:T(512)S(1)} fusion(s32[]{:T(128)} %bitcast.9, s32[]{:T(128)} %bitcast.8), kind=kLoop, calls=%fused_computation.44 | loop fusion | flops 2560 | bytes 2056 | tf_op jit(solution)/shard_map/jit(_where)/select_n | solution.py:41
  23.8 7.3 %collective-permute-done = bf16[512,1,128]{0,2,1:T(8,128)(2,1)S(1)} collective-permute-done((bf16[512,1,128]{0,2,1:T(8,128)(2,1)S(1)}, bf16[512,1,128]{0,2,1:T(8,128)(2,1)S(1)}, u32[]{:S(2)}, u32[]{:S(2)}) %collective-permute-start) | collective-permute-done | bytes 131104 | tf_op jit(solution)/shard_map/ppermute | solution.py:10
  31.1 1.9 %collective-permute-start.1 = (bf16[512,1,128]{0,2,1:T(8,128)(2,1)S(1)}, bf16[512,1,128]{0,2,1:T(8,128)(2,1)S(1)}, u32[]{:S(2)}, u32[]{:S(2)}) collective-permute-start(bf16[512,1,128]{0,2,1:T(8,128)(2,1)S(1)} %collective-permute-done), channel_id=1, source_target_pairs={{764,0},{0,4},{4,8},{8,12},{12,16},{16,20},{20,24},{24,28},{28,32}... | collective-permute-start | bytes 393224 | tf_op jit(solution)/shard_map/ppermute | solution.py:10
  33.1 1.2 %collective-permute-done.2 = bf16[512,1,128]{2,0,1:T(8,128)(2,1)S(1)} collective-permute-done((bf16[512,1,128]{2,0,1:T(8,128)(2,1)S(1)}, bf16[512,1,128]{2,0,1:T(8,128)(2,1)S(1)}, u32[]{:S(2)}, u32[]{:S(2)}) %collective-permute-start.2) | collective-permute-done | bytes 131104 | tf_op jit(solution)/shard_map/ppermute | solution.py:10
  34.4 1.9 %collective-permute-start.3 = (bf16[512,1,128]{2,0,1:T(8,128)(2,1)S(1)}, bf16[512,1,128]{2,0,1:T(8,128)(2,1)S(1)}, u32[]{:S(2)}, u32[]{:S(2)}) collective-permute-start(bf16[512,1,128]{2,0,1:T(8,128)(2,1)S(1)} %collective-permute-done.2), channel_id=1, source_target_pairs={{764,0},{0,4},{4,8},{8,12},{12,16},{16,20},{20,24},{24,28},{28,32}... | collective-permute-start | bytes 393224 | tf_op jit(solution)/shard_map/ppermute | solution.py:10
  36.3 7.5 %collective-permute-done.1 = bf16[512,1,128]{0,2,1:T(8,128)(2,1)S(1)} collective-permute-done((bf16[512,1,128]{0,2,1:T(8,128)(2,1)S(1)}, bf16[512,1,128]{0,2,1:T(8,128)(2,1)S(1)}, u32[]{:S(2)}, u32[]{:S(2)}) %collective-permute-start.1) | collective-permute-done | bytes 131104 | tf_op jit(solution)/shard_map/ppermute | solution.py:10
  43.8 0.2 copy.16
  44.0 2.1 %collective-permute-done.3 = bf16[512,1,128]{2,0,1:T(8,128)(2,1)S(1)} collective-permute-done((bf16[512,1,128]{2,0,1:T(8,128)(2,1)S(1)}, bf16[512,1,128]{2,0,1:T(8,128)(2,1)S(1)}, u32[]{:S(2)}, u32[]{:S(2)}) %collective-permute-start.3) | collective-permute-done | bytes 131104 | tf_op jit(solution)/shard_map/ppermute | solution.py:10
  46.2 9.0 %while.11 = (s32[]{:T(128)}, bf16[4,512,1,128]{3,1,2,0:T(8,128)(2,1)S(1)}, bf16[4,512,1,128]{1,3,0,2:T(8,128)(2,1)S(1)}, bf16[1536,1,128]{2,0,1:T(8,128)(2,1)S(1...) while((s32[]{:T(128)}, ...), condition=%wide.region_5.6_spmd.clone, body=%wide.region_2.5_spmd.clone.sunk | while | flops 409795584 | bytes 10506333 | solution.py:64
  46.2 0.9 %fusion.41 = (f32[512]{0:T(512)S(1)}, f32[512,1536]{1,0:T(8,128)S(1)}) fusion(bf16[1536,1,128]{2,0,1:T(8,128)(2,1)S(1)} %get-tuple-element.180, bf16[4,512,1,128]{1,3,0,2:T(8,128)(2,1)S(1)} %get-tuple-element.179, s32[]{:T(128)} %get-tuple-element.169, s32[512]{0:T(512)S(1)} %get-tuple-element.182, s32[1536]{0:T(1024)S(1)} %get-tuple-element.183), kind=kOutput, calls=%fused_computation.50.clone.1 | convolution fusion | flops 204471808 | bytes 3682308 | tf_op jit(solution)/shard_map/while/body/eval_jaxpr/qkd,skd->kqs/dot_general | solution.py:52
  47.1 0.6 fusion.42
  47.6 0.8 %fusion.43 = bf16[4,512,1,128]{3,1,2,0:T(8,128)(2,1)S(1)} fusion(bf16[4,512,1,128]{3,1,2,0:T(8,128)(2,1)S(1)} %get-tuple-element.170, s32[]{:T(128)} %get-tuple-element.169, f32[512,1536]{1,0:T(8,128)S(1)} %get-tuple-element.159, f32[512]{0:T(512)S(1)} %fusion.42, f32[512]{0:T(512)S(1)} %get-tuple-element.160, ...), kind=kOutput, calls=%fused_computation.9.clone.1 | convolution fusion | flops 203751424 | bytes 3674116 | tf_op jit(solution)/shard_map/while/body/eval_jaxpr/kqs,skd->qkd/dot_general | solution.py:59
  48.4 0.9 %fusion.41 = (f32[512]{0:T(512)S(1)}, f32[512,1536]{1,0:T(8,128)S(1)}) fusion(bf16[1536,1,128]{2,0,1:T(8,128)(2,1)S(1)} %get-tuple-element.180, bf16[4,512,1,128]{1,3,0,2:T(8,128)(2,1)S(1)} %get-tuple-element.179, s32[]{:T(128)} %get-tuple-element.169, s32[512]{0:T(512)S(1)} %get-tuple-element.182, s32[1536]{0:T(1024)S(1)} %get-tuple-element.183), kind=kOutput, calls=%fused_computation.50.clone.1 | convolution fusion | flops 204471808 | bytes 3682308 | tf_op jit(solution)/shard_map/while/body/eval_jaxpr/qkd,skd->kqs/dot_general | solution.py:52
  49.3 0.6 fusion.42
  49.9 0.8 %fusion.43 = bf16[4,512,1,128]{3,1,2,0:T(8,128)(2,1)S(1)} fusion(bf16[4,512,1,128]{3,1,2,0:T(8,128)(2,1)S(1)} %get-tuple-element.170, s32[]{:T(128)} %get-tuple-element.169, f32[512,1536]{1,0:T(8,128)S(1)} %get-tuple-element.159, f32[512]{0:T(512)S(1)} %fusion.42, f32[512]{0:T(512)S(1)} %get-tuple-element.160, ...), kind=kOutput, calls=%fused_computation.9.clone.1 | convolution fusion | flops 203751424 | bytes 3674116 | tf_op jit(solution)/shard_map/while/body/eval_jaxpr/kqs,skd->qkd/dot_general | solution.py:59
  50.7 0.9 %fusion.41 = (f32[512]{0:T(512)S(1)}, f32[512,1536]{1,0:T(8,128)S(1)}) fusion(bf16[1536,1,128]{2,0,1:T(8,128)(2,1)S(1)} %get-tuple-element.180, bf16[4,512,1,128]{1,3,0,2:T(8,128)(2,1)S(1)} %get-tuple-element.179, s32[]{:T(128)} %get-tuple-element.169, s32[512]{0:T(512)S(1)} %get-tuple-element.182, s32[1536]{0:T(1024)S(1)} %get-tuple-element.183), kind=kOutput, calls=%fused_computation.50.clone.1 | convolution fusion | flops 204471808 | bytes 3682308 | tf_op jit(solution)/shard_map/while/body/eval_jaxpr/qkd,skd->kqs/dot_general | solution.py:52
  51.6 0.6 fusion.42
  52.2 0.8 %fusion.43 = bf16[4,512,1,128]{3,1,2,0:T(8,128)(2,1)S(1)} fusion(bf16[4,512,1,128]{3,1,2,0:T(8,128)(2,1)S(1)} %get-tuple-element.170, s32[]{:T(128)} %get-tuple-element.169, f32[512,1536]{1,0:T(8,128)S(1)} %get-tuple-element.159, f32[512]{0:T(512)S(1)} %fusion.42, f32[512]{0:T(512)S(1)} %get-tuple-element.160, ...), kind=kOutput, calls=%fused_computation.9.clone.1 | convolution fusion | flops 203751424 | bytes 3674116 | tf_op jit(solution)/shard_map/while/body/eval_jaxpr/kqs,skd->qkd/dot_general | solution.py:59
  53.0 0.9 %fusion.41 = (f32[512]{0:T(512)S(1)}, f32[512,1536]{1,0:T(8,128)S(1)}) fusion(bf16[1536,1,128]{2,0,1:T(8,128)(2,1)S(1)} %get-tuple-element.180, bf16[4,512,1,128]{1,3,0,2:T(8,128)(2,1)S(1)} %get-tuple-element.179, s32[]{:T(128)} %get-tuple-element.169, s32[512]{0:T(512)S(1)} %get-tuple-element.182, s32[1536]{0:T(1024)S(1)} %get-tuple-element.183), kind=kOutput, calls=%fused_computation.50.clone.1 | convolution fusion | flops 204471808 | bytes 3682308 | tf_op jit(solution)/shard_map/while/body/eval_jaxpr/qkd,skd->kqs/dot_general | solution.py:52
  53.8 0.6 fusion.42
  54.4 0.8 %fusion.43 = bf16[4,512,1,128]{3,1,2,0:T(8,128)(2,1)S(1)} fusion(bf16[4,512,1,128]{3,1,2,0:T(8,128)(2,1)S(1)} %get-tuple-element.170, s32[]{:T(128)} %get-tuple-element.169, f32[512,1536]{1,0:T(8,128)S(1)} %get-tuple-element.159, f32[512]{0:T(512)S(1)} %fusion.42, f32[512]{0:T(512)S(1)} %get-tuple-element.160, ...), kind=kOutput, calls=%fused_computation.9.clone.1 | convolution fusion | flops 203751424 | bytes 3674116 | tf_op jit(solution)/shard_map/while/body/eval_jaxpr/kqs,skd->qkd/dot_general | solution.py:59
  55.2 0.4 copy.17
  55.6 0.2 all_to_all.14
  55.8 18.2 %all_to_all.19 = bf16[4,128,512]{2,1,0:T(8,128)(2,1)S(1)} all-to-all(bf16[4,128,512]{2,1,0:T(8,128)(2,1)S(1)} %all_to_all.14), channel_id=1, replica_groups=mesh['ctx'=192,'head'=4] {'head'}, dimensions={0} | all-to-all | bytes 1048576 | tf_op jit(solution)/shard_map/all_to_all | solution.py:91
  74.0 0.3 copy.18
  74.3 1.0 %copy.19 = bf16[128,2048]{1,0:T(8,128)(2,1)} copy(bf16[128,2048]{0,1:T(8,128)(2,1)S(1)} %bitcast.63) | data formatting | bytes 1048576 | tf_op jit(solution)/shard_map/all_to_all | solution.py:91
  (15 shorter events, 0.1 us)
Async XLA Ops:
  0.0 1.5 %copy-start = (bf16[4096,128]{1,0:T(8,128)(2,1)S(1)}, bf16[4096,128]{1,0:T(8,128)(2,1)}, u32[]{:S(2)}) copy-start(bf16[4096,128]{1,0:T(8,128)(2,1)} %param.11) | copy-start | bytes 3145732
  1.5 5.2 %copy-start.2 = (f32[128]{0:T(128)S(1)}, f32[128]{0:T(128)}, u32[]{:S(2)}) copy-start(f32[128]{0:T(128)} %param.14) | copy-start | bytes 1540
  1.5 10.0 %copy-start.1 = (bf16[512,4096]{1,0:T(8,128)(2,1)S(1)}, bf16[512,4096]{1,0:T(8,128)(2,1)}, u32[]{:S(2)}) copy-start(bf16[512,4096]{1,0:T(8,128)(2,1)} %param.9) | copy-start | bytes 12582916
  1.5 10.0 %copy-start.5 = (bf16[4096,128]{1,0:T(8,128)(2,1)S(1)}, bf16[4096,128]{1,0:T(8,128)(2,1)}, u32[]{:S(2)}) copy-start(bf16[4096,128]{1,0:T(8,128)(2,1)} %param.12) | copy-start | bytes 3145732
  6.9 11.0 %copy-start.4 = (bf16[4096,512]{1,0:T(8,128)(2,1)S(1)}, bf16[4096,512]{1,0:T(8,128)(2,1)}, u32[]{:S(2)}) copy-start(bf16[4096,512]{1,0:T(8,128)(2,1)} %param.10) | copy-start | bytes 12582916
  7.5 23.7 %collective-permute-start = (bf16[512,1,128]{0,2,1:T(8,128)(2,1)S(1)}, bf16[512,1,128]{0,2,1:T(8,128)(2,1)S(1)}, u32[]{:S(2)}, u32[]{:S(2)}) collective-permute-start(bf16[512,1,128]{0,2,1:T(8,128)(2,1)S(1)} %pad_maximum_fusion.2), channel_id=1, source_target_pairs={{764,0},{0,4},{4,8},{8,12},{12,16},{16,20},{20,24},{24,28},{28,32}... | collective-permute-start | bytes 393224 | tf_op jit(solution)/shard_map/ppermute | solution.py:10
  12.8 21.5 %collective-permute-start.2 = (bf16[512,1,128]{2,0,1:T(8,128)(2,1)S(1)}, bf16[512,1,128]{2,0,1:T(8,128)(2,1)S(1)}, u32[]{:S(2)}, u32[]{:S(2)}) collective-permute-start(bf16[512,1,128]{2,0,1:T(8,128)(2,1)S(1)} %fusion.13), channel_id=1, source_target_pairs={{764,0},{0,4},{4,8},{8,12},{12,16},{16,20},{20,24},{24,28},{28,32}... | collective-permute-start | bytes 393224 | tf_op jit(solution)/shard_map/ppermute | solution.py:10
  17.8 3.1 %copy-start.3 = (f32[128]{0:T(128)S(1)}, f32[128]{0:T(128)}, u32[]{:S(2)}) copy-start(f32[128]{0:T(128)} %param.13) | copy-start | bytes 1540
  31.1 12.7 %collective-permute-start.1 = (bf16[512,1,128]{0,2,1:T(8,128)(2,1)S(1)}, bf16[512,1,128]{0,2,1:T(8,128)(2,1)S(1)}, u32[]{:S(2)}, u32[]{:S(2)}) collective-permute-start(bf16[512,1,128]{0,2,1:T(8,128)(2,1)S(1)} %collective-permute-done), channel_id=1, source_target_pairs={{764,0},{0,4},{4,8},{8,12},{12,16},{16,20},{20,24},{24,28},{28,32}... | collective-permute-start | bytes 393224 | tf_op jit(solution)/shard_map/ppermute | solution.py:10
  34.4 11.8 %collective-permute-start.3 = (bf16[512,1,128]{2,0,1:T(8,128)(2,1)S(1)}, bf16[512,1,128]{2,0,1:T(8,128)(2,1)S(1)}, u32[]{:S(2)}, u32[]{:S(2)}) collective-permute-start(bf16[512,1,128]{2,0,1:T(8,128)(2,1)S(1)} %collective-permute-done.2), channel_id=1, source_target_pairs={{764,0},{0,4},{4,8},{8,12},{12,16},{16,20},{20,24},{24,28},{28,32}... | collective-permute-start | bytes 393224 | tf_op jit(solution)/shard_map/ppermute | solution.py:10
where the time goes:
time: 75.6 us; the launch traced here: 75.3 us
  blocking collectives  18.2 us (24%)
  waiting for transfers between devices  18.1 us (24%)
  matrix products  14.2 us (19%)
  starting transfers between devices  11 us (15%)
  other arithmetic  9.16 us (12%)
  local copies, waits for them, and re-layouts  4.29 us (6%)
    all_to_all x1, blocking collectives, shards(): lax.all_to_all(attended, 'head', split_axis=0, concat_axis=1, tiled=True)  18.2 us
    ppermute x4, waiting for transfers between devices, from_behind(): return lax.ppermute(block, axis, route)  18.1 us
    ppermute x4, starting transfers between devices, from_behind(): return lax.ppermute(block, axis, route)  11 us
    dot_general x2, matrix products, projected_rows(): rows = jnp.dot(hidden, weight, preferred_element_type=jnp.float32)  6.25 us
    select_n x3, other arithmetic, block_positions(): jnp.where(offsets < half_len, pair[0] + offsets, pair[1] + offsets - half...  3.88 us
    dot_general x4, matrix products, one_member(): jnp.einsum('qkd,skd->kqs', member, key_rows, preferred_element_type=jnp.f...  3.57 us
    dot_general x4, matrix products, one_member(): jnp.einsum('kqs,skd->qkd', weights, value_rows, preferred_element_type=jn...  3.1 us
    reduce_sum x4, other arithmetic, one_member(): jnp.sum(weights, axis=-1, keepdims=True)  2.29 us
  transfers between devices with their start and end apart: 4, of which 4 were waited for; matrix products, arithmetic and copies ran while one was open for 12% of the time, Pallas kernels for 0%

commit v1 on v0

v1 whole, which is shorter than its diff:
```python
import functools

import jax
import jax.numpy as jnp
import numpy as np
from jax import lax
from jax.experimental import pallas as pl
from jax.experimental.pallas import tpu as pltpu
from jax.sharding import PartitionSpec as P

MESH = pl.DeviceIdType.MESH
NEG = -1e30
F32 = jnp.float32
BF16 = jnp.bfloat16


def half_pi_parts():
    rest, parts = np.pi / 2, []
    for _ in range(3):
        unit = 2.0 ** (np.floor(np.log2(rest)) - 7)
        parts.append(float(np.floor(rest / unit) * unit))
        rest -= parts[-1]
    return parts + [float(np.float32(rest))]


def cos_sin(angle, is_cos):
    turns = jnp.floor(angle * np.float32(2 / np.pi) + 0.5)
    r = angle
    for part in half_pi_parts():
        r = r - turns * np.float32(part)
    r2 = r * r
    s = r + r * r2 * (
        np.float32(-1.6666654611e-1)
        + r2 * (np.float32(8.3321608736e-3) + r2 * np.float32(-1.9515295891e-4))
    )
    c = 1.0 - 0.5 * r2 + r2 * r2 * (
        np.float32(4.166664568298827e-2)
        + r2 * (np.float32(-1.388731625493765e-3) + r2 * np.float32(2.443315711809948e-5))
    )
    quadrant = turns.astype(jnp.int32) + jnp.where(is_cos, 0, 3)
    value = jnp.where((quadrant & 1) == 0, c, s)
    return jnp.where(((quadrant + 1) & 2) == 0, value, -value)


def kernel(
    n_ctx, hid, wq, wk, wv, gq, gk, freq, starts, out,
    hbuf, wqb, wkvb, cosb, sinb, kv, q, acc, top, tot, att,
    in_sem, kv_send, kv_recv, out_send, out_recv, own_sem,
):
    c = lax.axis_index("ctx")
    h = lax.axis_index("head")
    blk, width = hid.shape
    half = blk // 2
    heads = wq.shape[1] // 128
    rows = blk // 4
    grp = heads * rows
    chunks = 4
    step = width // chunks

    def ctx_at(d):
        return lax.rem(c + (d + n_ctx), n_ctx)

    y_hi, core = h // 2, lax.rem(h, 2)
    far_same = (1 - y_hi) * 2 + core
    far_other = (1 - y_hi) * 2 + 1 - core
    near_other = y_hi * 2 + 1 - core
    peers = (far_same, far_other, near_other)

    barrier = pltpu.get_barrier_semaphore()
    for d in (1, 2, -1, -2):
        pl.semaphore_signal(barrier, inc=1, device_id=(ctx_at(d), h), device_id_type=MESH)
    for peer in peers:
        pl.semaphore_signal(barrier, inc=1, device_id=(c, peer), device_id_type=MESH)

    loads = []
    for i in range(chunks):
        part = pl.ds(i * step, step)
        loads.append([
            pltpu.make_async_copy(hid.at[:, part], hbuf.at[:, part], in_sem.at[4 * i]),
            pltpu.make_async_copy(wk.at[part], wkvb.at[part, pl.ds(0, 128)], in_sem.at[4 * i + 1]),
            pltpu.make_async_copy(wv.at[part], wkvb.at[part, pl.ds(128, 128)], in_sem.at[4 * i + 2]),
        ])
    q_loads = [
        pltpu.make_async_copy(
            wq.at[pl.ds(i * step, step)], wqb.at[pl.ds(i * step, step)], in_sem.at[4 * i + 3]
        )
        for i in range(chunks)
    ]
    for group in loads:
        for load in group:
            load.start()
    for load in q_loads:
        load.start()

    lane = lax.broadcasted_iota(jnp.int32, (blk, 128), 1)
    token = lax.broadcasted_iota(jnp.int32, (blk, 128), 0)
    start = [starts[2 * c], starts[2 * c + 1]]
    pos = jnp.where(token < half, start[0] + token, start[1] + token - half)
    first = lane < 64
    table = cos_sin(pos.astype(F32) * freq[...], first)
    turned = pltpu.roll(table, 64, 1)
    cosb[...] = jnp.where(first, table, turned)
    sinb[...] = jnp.where(first, -turned, table)

    def normed(x, gain):
        x = x * lax.rsqrt(jnp.mean(x * x, axis=-1, keepdims=True) + 1e-6) * gain
        return x * cosb[...] + pltpu.roll(x, 64, 1) * sinb[...]

    total = None
    for i in range(chunks):
        for load in loads[i]:
            load.wait()
        part = pl.ds(i * step, step)
        term = jnp.dot(hbuf[:, part], wkvb[part, :], preferred_element_type=F32)
        total = term if total is None else total + term
    kv[0, 1] = total[:, 128:].astype(BF16)
    kv[0, 0] = normed(total[:, :128], gk[...]).astype(BF16)

    pl.semaphore_wait(barrier, 7)
    kv_copies = {}
    for d in (1, 2):
        for s in (0, 1):
            i = 2 * (d - 1) + s
            kv_copies[d, s] = pltpu.make_async_remote_copy(
                src_ref=kv.at[0, s],
                dst_ref=kv.at[d, s],
                send_sem=kv_send.at[i],
                recv_sem=kv_recv.at[i],
                device_id=(ctx_at(d), h),
                device_id_type=MESH,
            )
            kv_copies[d, s].start()

    qsum = None
    for i in range(chunks):
        q_loads[i].wait()
        part = pl.ds(i * step, step)
        term = jnp.dot(hbuf[:, part], wqb[part, :], preferred_element_type=F32)
        qsum = term if qsum is None else qsum + term
    for j in range(heads):
        rotated = normed(qsum[:, j * 128 : (j + 1) * 128], gq[...]).astype(BF16)
        for g in range(4):
            q[pl.ds(g * grp + j * rows, rows), :] = rotated[g * rows : (g + 1) * rows]

    factor = np.float32(128 ** (-0.5) * np.log2(np.e))
    tiles = blk // 128

    def scores(g, d):
        return lax.dot_general(
            q[pl.ds(g * grp, grp), :], kv[d, 0], (((1,), (1,)), ((), ())),
            preferred_element_type=F32,
        )

    def lane_fold(op, x):
        folded = x[:, :128]
        for i in range(1, tiles):
            folded = op(folded, x[:, i * 128 : (i + 1) * 128])
        return folded

    def weigh(p, d):
        return jnp.dot(p.astype(BF16), kv[d, 1], preferred_element_type=F32)

    def q_start(g):
        return jnp.where(g < 2, start[0], start[1])

    def own(g, _):
        at = pl.ds(pl.multiple_of(g * grp, grp), grp)
        s = scores(g, 0)
        key = lax.broadcasted_iota(jnp.int32, (rows, blk), 1)
        k_pos = jnp.where(key < half, start[0] + key, start[1] + key - half)
        q_pos = q_start(g) + lax.rem(g, 2) * rows + lax.broadcasted_iota(jnp.int32, (rows, blk), 0)
        seen = k_pos <= q_pos
        for j in range(heads):
            a = pl.ds(pl.multiple_of(g * grp + j * rows, rows), rows)
            sj = jnp.where(seen, s[j * rows : (j + 1) * rows], NEG)
            m = jnp.max(lane_fold(jnp.maximum, sj), axis=-1, keepdims=True)
            p = jnp.exp2((sj - m) * factor)
            top[a, :] = jnp.broadcast_to(m, (rows, 128))
            tot[a, :] = lane_fold(jnp.add, p)
            acc[a, :] = weigh(p, 0)
        return 0

    def biases(g, d):
        return [
            jnp.where(starts[2 * ctx_at(-d) + i] <= q_start(g), np.float32(0), np.float32(NEG))
            for i in range(2)
        ]

    def further(g, d, finish):
        s = scores(g, d)
        bias = biases(g, d)
        for j in range(heads):
            a = pl.ds(pl.multiple_of(g * grp + j * rows, rows), rows)
            sj = s[j * rows : (j + 1) * rows]
            left, right = sj[:, :half], sj[:, half:]
            peak = jnp.maximum(
                jnp.maximum(left[:, :128], left[:, 128:]) + bias[0],
                jnp.maximum(right[:, :128], right[:, 128:]) + bias[1],
            )
            old = top[a, :]
            new = jnp.maximum(old, jnp.max(peak, axis=-1, keepdims=True))
            m = new[:, :1]
            p = jnp.concatenate(
                [jnp.exp2((left - (m - bias[0])) * factor), jnp.exp2((right - (m - bias[1])) * factor)],
                axis=1,
            )
            keep = jnp.exp2((old - new) * factor)
            tot_new = tot[a, :] * keep + lane_fold(jnp.add, p)
            acc_new = acc[a, :] * keep + weigh(p, d)
            if finish is None:
                top[a, :], tot[a, :], acc[a, :] = new, tot_new, acc_new
            else:
                denom = jnp.sum(tot_new, axis=-1, keepdims=True)
                finish(j, (acc_new / denom).astype(BF16))

    lax.fori_loop(0, 4, own, 0)

    kv_copies[1, 0].wait_recv()
    kv_copies[1, 1].wait_recv()

    def near(g, _):
        further(g, 1, None)
        return 0

    lax.fori_loop(0, 4, near, 0)

    kv_copies[2, 0].wait_recv()
    kv_copies[2, 1].wait_recv()
    mine = pl.ds(pl.multiple_of(h * heads * 128, heads * 128), heads * 128)

    def target(t):
        return jnp.where(t == 0, far_same, jnp.where(t == 1, far_other, jnp.where(t == 2, near_other, h)))

    def result_copy(t):
        return pltpu.make_async_remote_copy(
            src_ref=att.at[t],
            dst_ref=out.at[:, mine],
            send_sem=out_send.at[t],
            recv_sem=out_recv.at[t],
            device_id=(c, target(t)),
            device_id_type=MESH,
        )

    def last(t, _):
        def finish(j, value):
            att[t, :, j * 128 : (j + 1) * 128] = value

        further(target(t), 2, finish)

        @pl.when(t < 3)
        def _():
            result_copy(t).start()

        return 0

    lax.fori_loop(0, 4, last, 0)
    own_copy = pltpu.make_async_copy(att.at[3], out.at[:, mine], own_sem)
    own_copy.start()
    for copy in kv_copies.values():
        copy.wait_send()
    own_copy.wait()
    for t in range(3):
        result_copy(jnp.int32(t)).wait()


def solution(mesh):
    n_ctx = mesh.shape["ctx"]

    def shards(hidden, w_query, key_projection, value_projection, q_gain, key_norm_gain, starts):
        blk, width = hidden.shape
        cols = w_query.shape[1]
        rows = blk // 4
        freqs = jnp.power(F32(1000000.0), -jnp.arange(64, dtype=F32) * 2.0 / 128)
        freqs = jnp.concatenate([freqs, freqs]).reshape(1, 128)
        any_ = pl.BlockSpec(memory_space=pl.ANY)
        vmem = pl.BlockSpec(memory_space=pltpu.VMEM)
        n_rows = rows * 4 * (cols // 128)
        return pl.pallas_call(
            functools.partial(kernel, n_ctx),
            out_shape=jax.ShapeDtypeStruct((rows, cols * 4), BF16),
            in_specs=[any_] * 4 + [vmem] * 3 + [pl.BlockSpec(memory_space=pltpu.SMEM)],
            out_specs=any_,
            scratch_shapes=[
                pltpu.VMEM((blk, width), BF16),
                pltpu.VMEM((width, cols), BF16),
                pltpu.VMEM((width, 256), BF16),
                pltpu.VMEM((blk, 128), F32),
                pltpu.VMEM((blk, 128), F32),
                pltpu.VMEM((3, 2, blk, 128), BF16),
                pltpu.VMEM((n_rows, 128), BF16),
                pltpu.VMEM((n_rows, 128), F32),
                pltpu.VMEM((n_rows, 128), F32),
                pltpu.VMEM((n_rows, 128), F32),
                pltpu.VMEM((4, rows, cols), BF16),
                pltpu.SemaphoreType.DMA((16,)),
                pltpu.SemaphoreType.DMA((4,)),
                pltpu.SemaphoreType.DMA((4,)),
                pltpu.SemaphoreType.DMA((3,)),
                pltpu.SemaphoreType.DMA((3,)),
                pltpu.SemaphoreType.DMA,
            ],
            compiler_params=pltpu.CompilerParams(
                collective_id=0, has_side_effects=True, vmem_limit_bytes=60 << 20
            ),
        )(
            hidden, w_query, key_projection, value_projection,
            q_gain.reshape(1, 128), key_norm_gain.reshape(1, 128), freqs, starts,
        )

    return jax.shard_map(
        shards,
        mesh=mesh,
        in_specs=(P("ctx", None), P(None, "head"), P(None, "head"), P(None, "head"), P(), P(), P()),
        out_specs=P(("ctx", "head"), None),
        check_vma=False,
    )
```

time: 75.6 us -> 55 us (0.73)
  the two profiles are of different devices: /device:TPU:1 before, /device:TPU:3 now
where the time goes in v1:
time: 55 us; the launch traced here: 54.8 us
  Pallas kernels  52.3 us (95%)
  local copies, waits for them, and re-layouts  1.88 us (3%)
  other arithmetic  0.6 us (1%)
    pallas_call x1, Pallas kernels, shards(): pl.pallas_call(functools.partial(kernel, n_ctx), out_shape=jax.ShapeDtype...  52.3 us
    unnamed x1, local copies, waits for them, and re-layouts  1.88 us

profile of v1, /device:TPU:3, one launch (start us, length us, event | category | flops | bytes accessed | tf_op | source)
XLA Modules:
  0.0 54.8 jit_solution(13540861087654037303)
XLA Ops:
  0.0 0.6 %maximum_bitcast_fusion.freq = f32[1,128]{1,0:T(1,128)} fusion(f32[64]{0:T(128)S(1)} %multiply_power_fusion), kind=kLoop, calls=%fused_computation | loop fusion | flops 128 | bytes 768 | tf_op jit(solution)/shard_map/reshape | solution.py:274
  0.6 52.3 %shard_map.73 = bf16[128,2048]{1,0:T(8,128)(2,1)} custom-call(bf16[512,4096]{1,0:T(8,128)(2,1)} %hid.1, bf16[4096,512]{1,0:T(8,128)(2,1)} %wq.1, bf16[4096,128]{1,0:T(8,128)(2,1)} %wk.1, bf16[4096,128]{1,0:T(8,128)(2,1)} %wv.1, f32[1,128]{1,0:T(1,128)} %bitcast.4, f32[1,128]{1,0:T(1,128)} %bitcast.5, f32[1,128]{1,0:T(1,128)} %maximum_bitcast_fusion.freq, ...), custom_call_target="tpu_custom_call" | custom-call | tf_op jit(solution)/shard_map/pallas_call | solution.py:278
  52.9 1.9 %copy.9 = bf16[128,2048]{1,0:T(8,128)(2,1)} copy(bf16[128,2048]{1,0:T(8,128)(2,1)} %shard_map.73) | data formatting | bytes 1048576
  (1 shorter events, 0.0 us)

commit v2 on v1

v2 whole, which is shorter than its diff:
```python
import functools

import jax
import jax.numpy as jnp
import numpy as np
from jax import lax
from jax.experimental import pallas as pl
from jax.experimental.pallas import tpu as pltpu
from jax.sharding import PartitionSpec as P

MESH = pl.DeviceIdType.MESH
NEG = -1e30
F32 = jnp.float32
BF16 = jnp.bfloat16


def half_pi_parts():
    rest, parts = np.pi / 2, []
    for _ in range(3):
        unit = 2.0 ** (np.floor(np.log2(rest)) - 7)
        parts.append(float(np.floor(rest / unit) * unit))
        rest -= parts[-1]
    return parts + [float(np.float32(rest))]


def cos_sin(angle, is_cos):
    turns = jnp.floor(angle * np.float32(2 / np.pi) + 0.5)
    r = angle
    for part in half_pi_parts():
        r = r - turns * np.float32(part)
    r2 = r * r
    s = r + r * r2 * (
        np.float32(-1.6666654611e-1)
        + r2 * (np.float32(8.3321608736e-3) + r2 * np.float32(-1.9515295891e-4))
    )
    c = 1.0 - 0.5 * r2 + r2 * r2 * (
        np.float32(4.166664568298827e-2)
        + r2 * (np.float32(-1.388731625493765e-3) + r2 * np.float32(2.443315711809948e-5))
    )
    quadrant = turns.astype(jnp.int32) + jnp.where(is_cos, 0, 3)
    value = jnp.where((quadrant & 1) == 0, c, s)
    return jnp.where(((quadrant + 1) & 2) == 0, value, -value)


def kernel(
    n_ctx, hid, wq, wk, wv, gq, gk, freq, starts, out,
    hbuf, wqb, wkvb, cosb, sinb, kv, q, acc, top, tot, att,
    w_sem, h_sem, q_sem, kv_send, kv_recv, out_send, out_recv, own_sem,
):
    c = lax.axis_index("ctx")
    h = lax.axis_index("head")
    blk, width = hid.shape
    half = blk // 2
    heads = wq.shape[1] // 128
    rows = blk // 4
    grp = heads * rows
    chunks = 4
    step = width // chunks

    def ctx_at(d):
        return lax.rem(c + (d + n_ctx), n_ctx)

    x = lax.rem(c, 4)
    y_hi, core = h // 2, lax.rem(h, 2)
    peers = (
        (1 - y_hi) * 2 + core,
        (1 - y_hi) * 2 + 1 - core,
        y_hi * 2 + 1 - core,
        h,
    )

    barrier = pltpu.get_barrier_semaphore()
    for d in (-1, jnp.where(x == 0, 1, jnp.where(x == 1, -3, -2))):
        pl.semaphore_signal(barrier, inc=1, device_id=(ctx_at(d), h), device_id_type=MESH)
    for peer in peers[:3]:
        pl.semaphore_signal(barrier, inc=1, device_id=(c, peer), device_id_type=MESH)

    parts = [pl.ds(i * step, step) for i in range(chunks)]
    halves = [pl.ds(0, half), pl.ds(half, half)]
    w_loads = [
        (
            pltpu.make_async_copy(wk.at[part], wkvb.at[part, pl.ds(0, 128)], w_sem.at[2 * i]),
            pltpu.make_async_copy(wv.at[part], wkvb.at[part, pl.ds(128, 128)], w_sem.at[2 * i + 1]),
        )
        for i, part in enumerate(parts)
    ]
    h_loads = [
        [
            pltpu.make_async_copy(
                hid.at[tokens, part], hbuf.at[tokens, part], h_sem.at[n * chunks + i]
            )
            for i, part in enumerate(parts)
        ]
        for n, tokens in enumerate(halves)
    ]
    q_loads = [
        pltpu.make_async_copy(wq.at[part], wqb.at[part], q_sem.at[i])
        for i, part in enumerate(parts)
    ]
    for i in range(chunks):
        w_loads[i][0].start()
        w_loads[i][1].start()
        h_loads[0][i].start()
    for load in h_loads[1] + q_loads:
        load.start()

    lane = lax.broadcasted_iota(jnp.int32, (blk, 128), 1)
    token = lax.broadcasted_iota(jnp.int32, (blk, 128), 0)
    start = [starts[2 * c], starts[2 * c + 1]]
    pos = jnp.where(token < half, start[0] + token, start[1] + token - half)
    first = lane < 64
    table = cos_sin(pos.astype(F32) * freq[...], first)
    turned = pltpu.roll(table, 64, 1)
    cosb[...] = jnp.where(first, table, turned)
    sinb[...] = jnp.where(first, -turned, table)

    def normed(x, gain, tokens):
        x = x * lax.rsqrt(jnp.mean(x * x, axis=-1, keepdims=True) + 1e-6) * gain
        return x * cosb[tokens, :] + pltpu.roll(x, 64, 1) * sinb[tokens, :]

    def near_copy(n, s):
        i = 2 * n + s
        return pltpu.make_async_remote_copy(
            src_ref=kv.at[s, pl.ds(n * half, half)],
            dst_ref=kv.at[s, pl.ds(blk + n * half, half)],
            send_sem=kv_send.at[i],
            recv_sem=kv_recv.at[i],
            device_id=(ctx_at(1), h),
            device_id_type=MESH,
        )

    def second_copy(n, s):
        i = 2 * n + s
        over = (x == 2).astype(jnp.int32)
        return pltpu.make_async_remote_copy(
            src_ref=kv.at[s, pl.ds(n * half, half)],
            dst_ref=kv.at[s, pl.ds(pl.multiple_of((2 + over) * blk + n * half, half), half)],
            send_sem=kv_send.at[4 + i],
            recv_sem=kv_recv.at[4 + 4 * over + i],
            device_id=(ctx_at(2 + over), h),
            device_id_type=MESH,
        )

    def relay_copy(n, s):
        i = 2 * n + s
        held = 1 + 2 * x
        return pltpu.make_async_remote_copy(
            src_ref=kv.at[s, pl.ds(pl.multiple_of(held * blk + n * half, half), half)],
            dst_ref=kv.at[s, pl.ds(2 * blk + n * half, half)],
            send_sem=kv_send.at[8 + i],
            recv_sem=kv_recv.at[4 + i],
            device_id=(ctx_at(1 - 2 * x), h),
            device_id_type=MESH,
        )

    def arrival(slot, n, s):
        here = kv.at[s, pl.ds(slot * blk + n * half, half)]
        return pltpu.make_async_copy(here, here, kv_recv.at[4 * (slot - 1) + 2 * n + s])

    pieces = [(n, s) for n in (0, 1) for s in (1, 0)]
    for n, tokens in enumerate(halves):
        total = None
        for i, part in enumerate(parts):
            if n == 0:
                w_loads[i][0].wait()
                w_loads[i][1].wait()
            h_loads[n][i].wait()
            term = jnp.dot(hbuf[tokens, part], wkvb[part, :], preferred_element_type=F32)
            total = term if total is None else total + term
        kv[1, tokens, :] = total[:, 128:].astype(BF16)
        kv[0, tokens, :] = normed(total[:, :128], gk[...], tokens).astype(BF16)
        if n == 0:
            pl.semaphore_wait(barrier, 5 + (x == 1).astype(jnp.int32) - (x == 3).astype(jnp.int32))
        for s in (1, 0):
            near_copy(n, s).start()

            @pl.when(x < 3)
            def _():
                second_copy(n, s).start()

    qsum = None
    for i, part in enumerate(parts):
        q_loads[i].wait()
        term = jnp.dot(hbuf[:, part], wqb[part, :], preferred_element_type=F32)
        qsum = term if qsum is None else qsum + term
    everyone = pl.ds(0, blk)
    for j in range(heads):
        rotated = normed(qsum[:, j * 128 : (j + 1) * 128], gq[...], everyone).astype(BF16)
        for g in range(4):
            q[g * grp + j * rows : g * grp + (j + 1) * rows, :] = rotated[g * rows : (g + 1) * rows]

    factor = np.float32(128 ** (-0.5) * np.log2(np.e))
    contract_last = (((1,), (1,)), ((), ()))

    def lane_fold(op, x):
        folded = x[:, :128]
        for i in range(1, x.shape[1] // 128):
            folded = op(folded, x[:, i * 128 : (i + 1) * 128])
        return folded

    def q_start(t):
        return jnp.where((y_hi if t >= 2 else 1 - y_hi) == 0, start[0], start[1])

    for t in range(4):
        s = lax.dot_general(
            q[t * grp : (t + 1) * grp, :], kv[0, :blk, :], contract_last,
            preferred_element_type=F32,
        )
        key = lax.broadcasted_iota(jnp.int32, (rows, blk), 1)
        k_pos = jnp.where(key < half, start[0] + key, start[1] + key - half)
        q_pos = (
            start[t // 2]
            + (t % 2) * rows
            + lax.broadcasted_iota(jnp.int32, (rows, blk), 0)
        )
        seen = k_pos <= q_pos
        for j in range(heads):
            a = pl.ds(t * grp + j * rows, rows)
            sj = jnp.where(seen, s[j * rows : (j + 1) * rows], NEG)
            m = jnp.max(lane_fold(jnp.maximum, sj), axis=-1, keepdims=True)
            p = jnp.exp2((sj - m) * factor)
            top[a, :] = jnp.broadcast_to(m, (rows, 128))
            tot[a, :] = lane_fold(jnp.add, p)
            acc[a, :] = jnp.dot(p.astype(BF16), kv[1, :blk, :], preferred_element_type=F32)

    for piece in pieces:

        @pl.when(x == 0)
        def _():
            arrival(1, *piece).wait()

        @pl.when(x == 1)
        def _():
            arrival(3, *piece).wait()

        @pl.when(x < 2)
        def _():
            relay_copy(*piece).start()

    for piece in pieces:

        @pl.when(x > 0)
        def _():
            arrival(1, *piece).wait()

        arrival(2, *piece).wait()

    mine = h * heads * 128
    results = []
    for t in range(4):
        base = pl.multiple_of(peers[t] * grp, grp)
        s = lax.dot_general(
            q[pl.ds(base, grp), :], kv[0, blk : 3 * blk, :], contract_last,
            preferred_element_type=F32,
        )
        bias = [
            jnp.where(starts[2 * ctx_at(-d) + n] <= q_start(t), np.float32(0), np.float32(NEG))
            for d in (1, 2)
            for n in (0, 1)
        ]
        for j in range(heads):
            a = pl.ds(pl.multiple_of(base + j * rows, rows), rows)
            sj = s[j * rows : (j + 1) * rows]
            quarters = [sj[:, i * half : (i + 1) * half] for i in range(4)]
            peak = functools.reduce(
                jnp.maximum, [lane_fold(jnp.maximum, x) + b for x, b in zip(quarters, bias)]
            )
            old = top[a, :]
            new = jnp.maximum(old, jnp.max(peak, axis=-1, keepdims=True))
            m = new[:, :1]
            p = jnp.concatenate(
                [jnp.exp2((x - (m - b)) * factor) for x, b in zip(quarters, bias)], axis=1
            )
            keep = jnp.exp2((old - new) * factor)
            denom = jnp.sum(tot[a, :] * keep + lane_fold(jnp.add, p), axis=-1, keepdims=True)
            value = acc[a, :] * keep + jnp.dot(
                p.astype(BF16), kv[1, blk : 3 * blk, :], preferred_element_type=F32
            )
            att[t, :, j * 128 : (j + 1) * 128] = (value * (1.0 / denom)).astype(BF16)
            target = out.at[:, pl.ds(pl.multiple_of(mine + j * 128, 128), 128)]
            if t < 3:
                copy = pltpu.make_async_remote_copy(
                    src_ref=att.at[t, :, pl.ds(j * 128, 128)],
                    dst_ref=target,
                    send_sem=out_send.at[t * heads + j],
                    recv_sem=out_recv.at[t * heads + j],
                    device_id=(c, peers[t]),
                    device_id_type=MESH,
                )
            else:
                copy = pltpu.make_async_copy(
                    att.at[t, :, pl.ds(j * 128, 128)], target, own_sem.at[j]
                )
            copy.start()
            results.append(copy)
    for piece in pieces:
        near_copy(*piece).wait_send()

        @pl.when(x < 3)
        def _():
            second_copy(*piece).wait_send()

        @pl.when(x < 2)
        def _():
            relay_copy(*piece).wait_send()

    for copy in results:
        copy.wait()


def solution(mesh):
    n_ctx = mesh.shape["ctx"]

    def shards(hidden, w_query, key_projection, value_projection, q_gain, key_norm_gain, starts):
        blk, width = hidden.shape
        cols = w_query.shape[1]
        rows = blk // 4
        freqs = (1e6 ** (-np.arange(64) * 2.0 / 128)).astype(np.float32)
        freqs = jnp.asarray(np.tile(freqs, 2).reshape(1, 128))
        any_ = pl.BlockSpec(memory_space=pl.ANY)
        vmem = pl.BlockSpec(memory_space=pltpu.VMEM)
        n_rows = rows * 4 * (cols // 128)
        return pl.pallas_call(
            functools.partial(kernel, n_ctx),
            out_shape=pltpu.VMEM((rows, cols * 4), BF16),
            in_specs=[any_] * 4 + [vmem] * 3 + [pl.BlockSpec(memory_space=pltpu.SMEM)],
            out_specs=vmem,
            scratch_shapes=[
                pltpu.VMEM((blk, width), BF16),
                pltpu.VMEM((width, cols), BF16),
                pltpu.VMEM((width, 256), BF16),
                pltpu.VMEM((blk, 128), F32),
                pltpu.VMEM((blk, 128), F32),
                pltpu.VMEM((2, 4 * blk, 128), BF16),
                pltpu.VMEM((n_rows, 128), BF16),
                pltpu.VMEM((n_rows, 128), F32),
                pltpu.VMEM((n_rows, 128), F32),
                pltpu.VMEM((n_rows, 128), F32),
                pltpu.VMEM((4, rows, cols), BF16),
                pltpu.SemaphoreType.DMA((8,)),
                pltpu.SemaphoreType.DMA((8,)),
                pltpu.SemaphoreType.DMA((4,)),
                pltpu.SemaphoreType.DMA((12,)),
                pltpu.SemaphoreType.DMA((12,)),
                pltpu.SemaphoreType.DMA((12,)),
                pltpu.SemaphoreType.DMA((12,)),
                pltpu.SemaphoreType.DMA((4,)),
            ],
            compiler_params=pltpu.CompilerParams(
                collective_id=0, has_side_effects=True, vmem_limit_bytes=60 << 20
            ),
        )(
            hidden, w_query, key_projection, value_projection,
            q_gain.reshape(1, 128), key_norm_gain.reshape(1, 128), freqs, starts,
        )

    return jax.shard_map(
        shards,
        mesh=mesh,
        in_specs=(P("ctx", None), P(None, "head"), P(None, "head"), P(None, "head"), P(), P(), P()),
        out_specs=P(("ctx", "head"), None),
        check_vma=False,
    )
```

time: 55 us -> 44.9 us (0.82)
  the two profiles are of different devices: /device:TPU:3 before, /device:TPU:1 now
where the time goes in v2:
time: 44.9 us; the launch traced here: 44.4 us
  Pallas kernels  43.6 us (97%)
  local copies, waits for them, and re-layouts  0.8 us (2%)
    pallas_call x1, Pallas kernels, shards(): pl.pallas_call(functools.partial(kernel, n_ctx), out_shape=pltpu.VMEM((ro...  43.6 us

profile of v2, /device:TPU:1, one launch (start us, length us, event | category | flops | bytes accessed | tf_op | source)
XLA Modules:
  0.0 44.4 jit_solution(3378524678554528668)
XLA Ops:
  0.0 43.6 %shard_map.82 = bf16[128,2048]{1,0:T(8,128)(2,1)S(1)} custom-call(bf16[512,4096]{1,0:T(8,128)(2,1)} %hid.1, bf16[4096,512]{1,0:T(8,128)(2,1)} %wq.1, bf16[4096,128]{1,0:T(8,128)(2,1)} %wk.1, bf16[4096,128]{1,0:T(8,128)(2,1)} %wv.1, f32[1,128]{1,0:T(1,128)} %bitcast.2, f32[1,128]{1,0:T(1,128)} %bitcast.3, f32[1,128]{1,0:T(1,128)} %constant.2.clone.freq, ...), custom_call_target="tpu_custom_call" | custom-call | tf_op jit(solution)/shard_map/pallas_call | solution.py:323
  43.6 0.8 %copy.10 = bf16[128,2048]{1,0:T(8,128)(2,1)} copy(bf16[128,2048]{1,0:T(8,128)(2,1)S(1)} %shard_map.82) | data formatting | bytes 1048576

commit v3 on v2

--- a/solution.py
+++ b/solution.py
@@ -44,7 +44,7 @@
 
 def kernel(
     n_ctx, hid, wq, wk, wv, gq, gk, freq, starts, out,
-    hbuf, wqb, wkvb, cosb, sinb, kv, q, acc, top, tot, att,
+    hbuf, wqb, wkvb, cosb, sinb, kt, vb, q, acc, top, tot, att,
     w_sem, h_sem, q_sem, kv_send, kv_recv, out_send, out_recv, own_sem,
 ):
     c = lax.axis_index("ctx")
@@ -118,11 +118,15 @@
         x = x * lax.rsqrt(jnp.mean(x * x, axis=-1, keepdims=True) + 1e-6) * gain
         return x * cosb[tokens, :] + pltpu.roll(x, 64, 1) * sinb[tokens, :]
 
+    def held(s, at, size):
+        span = pl.ds(at if isinstance(at, int) else pl.multiple_of(at, size), size)
+        return vb.at[span] if s else kt.at[:, span]
+
     def near_copy(n, s):
         i = 2 * n + s
         return pltpu.make_async_remote_copy(
-            src_ref=kv.at[s, pl.ds(n * half, half)],
-            dst_ref=kv.at[s, pl.ds(blk + n * half, half)],
+            src_ref=held(s, n * rows, rows),
+            dst_ref=held(s, blk + n * rows, rows),
             send_sem=kv_send.at[i],
             recv_sem=kv_recv.at[i],
             device_id=(ctx_at(1), h),
@@ -133,31 +137,30 @@
         i = 2 * n + s
         over = (x == 2).astype(jnp.int32)
         return pltpu.make_async_remote_copy(
-            src_ref=kv.at[s, pl.ds(n * half, half)],
-            dst_ref=kv.at[s, pl.ds(pl.multiple_of((2 + over) * blk + n * half, half), half)],
-            send_sem=kv_send.at[4 + i],
-            recv_sem=kv_recv.at[4 + 4 * over + i],
+            src_ref=held(s, n * rows, rows),
+            dst_ref=held(s, (2 + over) * blk + n * rows, rows),
+            send_sem=kv_send.at[8 + i],
+            recv_sem=kv_recv.at[8 + 8 * over + i],
             device_id=(ctx_at(2 + over), h),
             device_id_type=MESH,
         )
 
     def relay_copy(n, s):
         i = 2 * n + s
-        held = 1 + 2 * x
         return pltpu.make_async_remote_copy(
-            src_ref=kv.at[s, pl.ds(pl.multiple_of(held * blk + n * half, half), half)],
-            dst_ref=kv.at[s, pl.ds(2 * blk + n * half, half)],
-            send_sem=kv_send.at[8 + i],
-            recv_sem=kv_recv.at[4 + i],
+            src_ref=held(s, (1 + 2 * x) * blk + n * rows, rows),
+            dst_ref=held(s, 2 * blk + n * rows, rows),
+            send_sem=kv_send.at[16 + i],
+            recv_sem=kv_recv.at[8 + i],
             device_id=(ctx_at(1 - 2 * x), h),
             device_id_type=MESH,
         )
 
     def arrival(slot, n, s):
-        here = kv.at[s, pl.ds(slot * blk + n * half, half)]
-        return pltpu.make_async_copy(here, here, kv_recv.at[4 * (slot - 1) + 2 * n + s])
-
-    pieces = [(n, s) for n in (0, 1) for s in (1, 0)]
+        here = held(s, slot * blk + n * rows, rows)
+        return pltpu.make_async_copy(here, here, kv_recv.at[8 * (slot - 1) + 2 * n + s])
+
+    pieces = [(n, s) for n in range(4) for s in (1, 0)]
     for n, tokens in enumerate(halves):
         total = None
         for i, part in enumerate(parts):
@@ -167,16 +170,16 @@
             h_loads[n][i].wait()
             term = jnp.dot(hbuf[tokens, part], wkvb[part, :], preferred_element_type=F32)
             total = term if total is None else total + term
-        kv[1, tokens, :] = total[:, 128:].astype(BF16)
-        kv[0, tokens, :] = normed(total[:, :128], gk[...], tokens).astype(BF16)
+        vb[tokens, :] = total[:, 128:].astype(BF16)
+        kt[:, tokens] = normed(total[:, :128], gk[...], tokens).T.astype(BF16)
         if n == 0:
             pl.semaphore_wait(barrier, 5 + (x == 1).astype(jnp.int32) - (x == 3).astype(jnp.int32))
-        for s in (1, 0):
-            near_copy(n, s).start()
+        for piece in pieces[4 * n : 4 * n + 4]:
+            near_copy(*piece).start()
 
             @pl.when(x < 3)
             def _():
-                second_copy(n, s).start()
+                second_copy(*piece).start()
 
     qsum = None
     for i, part in enumerate(parts):
@@ -190,7 +193,6 @@
             q[g * grp + j * rows : g * grp + (j + 1) * rows, :] = rotated[g * rows : (g + 1) * rows]
 
     factor = np.float32(128 ** (-0.5) * np.log2(np.e))
-    contract_last = (((1,), (1,)), ((), ()))
 
     def lane_fold(op, x):
         folded = x[:, :128]
@@ -198,30 +200,44 @@
             folded = op(folded, x[:, i * 128 : (i + 1) * 128])
         return folded
 
+    def weights(x, tops):
+        return jnp.concatenate(
+            [
+                jnp.exp2((x[:, i * 128 : (i + 1) * 128] - top_i) * factor)
+                for i, top_i in enumerate(tops)
+            ],
+            axis=1,
+        )
+
     def q_start(t):
         return jnp.where((y_hi if t >= 2 else 1 - y_hi) == 0, start[0], start[1])
 
+    triangle = lax.broadcasted_iota(jnp.int32, (rows, 128), 1) <= lax.broadcasted_iota(
+        jnp.int32, (rows, 128), 0
+    )
     for t in range(4):
-        s = lax.dot_general(
-            q[t * grp : (t + 1) * grp, :], kv[0, :blk, :], contract_last,
-            preferred_element_type=F32,
-        )
-        key = lax.broadcasted_iota(jnp.int32, (rows, blk), 1)
-        k_pos = jnp.where(key < half, start[0] + key, start[1] + key - half)
-        q_pos = (
-            start[t // 2]
-            + (t % 2) * rows
-            + lax.broadcasted_iota(jnp.int32, (rows, blk), 0)
-        )
-        seen = k_pos <= q_pos
+        mine, other = t // 2, 1 - t // 2
+        tiles = t % 2 + 1
+        bias = jnp.where(start[other] <= start[mine], np.float32(0), np.float32(NEG))
+        k_mine = slice(mine * half, mine * half + tiles * rows)
+        k_other = slice(other * half, (other + 1) * half)
+        s_mine = jnp.dot(q[t * grp : (t + 1) * grp, :], kt[:, k_mine], preferred_element_type=F32)
+        s_other = jnp.dot(q[t * grp : (t + 1) * grp, :], kt[:, k_other], preferred_element_type=F32)
         for j in range(heads):
             a = pl.ds(t * grp + j * rows, rows)
-            sj = jnp.where(seen, s[j * rows : (j + 1) * rows], NEG)
-            m = jnp.max(lane_fold(jnp.maximum, sj), axis=-1, keepdims=True)
-            p = jnp.exp2((sj - m) * factor)
-            top[a, :] = jnp.broadcast_to(m, (rows, 128))
-            tot[a, :] = lane_fold(jnp.add, p)
-            acc[a, :] = jnp.dot(p.astype(BF16), kv[1, :blk, :], preferred_element_type=F32)
+            sm = s_mine[j * rows : (j + 1) * rows]
+            so = s_other[j * rows : (j + 1) * rows]
+            edge = jnp.where(triangle, sm[:, -128:], NEG)
+            sm = edge if tiles == 1 else jnp.concatenate([sm[:, :128], edge], axis=1)
+            peak = jnp.maximum(lane_fold(jnp.maximum, sm), lane_fold(jnp.maximum, so) + bias)
+            m = jnp.broadcast_to(jnp.max(peak, axis=-1, keepdims=True), (rows, 128))
+            p_mine = weights(sm, [m] * tiles)
+            p_other = weights(so, [m - bias] * (half // 128))
+            top[a, :] = m
+            tot[a, :] = lane_fold(jnp.add, p_mine) + lane_fold(jnp.add, p_other)
+            acc[a, :] = jnp.dot(
+                p_mine.astype(BF16), vb[k_mine, :], preferred_element_type=F32
+            ) + jnp.dot(p_other.astype(BF16), vb[k_other, :], preferred_element_type=F32)
 
     for piece in pieces:
 
@@ -249,10 +265,7 @@
     results = []
     for t in range(4):
         base = pl.multiple_of(peers[t] * grp, grp)
-        s = lax.dot_general(
-            q[pl.ds(base, grp), :], kv[0, blk : 3 * blk, :], contract_last,
-            preferred_element_type=F32,
-        )
+        s = jnp.dot(q[pl.ds(base, grp), :], kt[:, blk : 3 * blk], preferred_element_type=F32)
         bias = [
             jnp.where(starts[2 * ctx_at(-d) + n] <= q_start(t), np.float32(0), np.float32(NEG))
             for d in (1, 2)
@@ -267,14 +280,11 @@
             )
             old = top[a, :]
             new = jnp.maximum(old, jnp.max(peak, axis=-1, keepdims=True))
-            m = new[:, :1]
-            p = jnp.concatenate(
-                [jnp.exp2((x - (m - b)) * factor) for x, b in zip(quarters, bias)], axis=1
-            )
+            p = weights(sj, [new - b for b in bias for _ in range(half // 128)])
             keep = jnp.exp2((old - new) * factor)
             denom = jnp.sum(tot[a, :] * keep + lane_fold(jnp.add, p), axis=-1, keepdims=True)
             value = acc[a, :] * keep + jnp.dot(
-                p.astype(BF16), kv[1, blk : 3 * blk, :], preferred_element_type=F32
+                p.astype(BF16), vb[blk : 3 * blk, :], preferred_element_type=F32
             )
             att[t, :, j * 128 : (j + 1) * 128] = (value * (1.0 / denom)).astype(BF16)
             target = out.at[:, pl.ds(pl.multiple_of(mine + j * 128, 128), 128)]
@@ -331,7 +341,8 @@
                 pltpu.VMEM((width, 256), BF16),
                 pltpu.VMEM((blk, 128), F32),
                 pltpu.VMEM((blk, 128), F32),
-                pltpu.VMEM((2, 4 * blk, 128), BF16),
+                pltpu.VMEM((128, 4 * blk), BF16),
+                pltpu.VMEM((4 * blk, 128), BF16),
                 pltpu.VMEM((n_rows, 128), BF16),
                 pltpu.VMEM((n_rows, 128), F32),
                 pltpu.VMEM((n_rows, 128), F32),
@@ -340,8 +351,8 @@
                 pltpu.SemaphoreType.DMA((8,)),
                 pltpu.SemaphoreType.DMA((8,)),
                 pltpu.SemaphoreType.DMA((4,)),
-                pltpu.SemaphoreType.DMA((12,)),
-                pltpu.SemaphoreType.DMA((12,)),
+                pltpu.SemaphoreType.DMA((24,)),
+                pltpu.SemaphoreType.DMA((24,)),
                 pltpu.SemaphoreType.DMA((12,)),
                 pltpu.SemaphoreType.DMA((12,)),
                 pltpu.SemaphoreType.DMA((4,)),

time: 44.9 us -> 44.6 us (level)
  no operation moved by 1% of the time
where the time goes in v3:
time: 44.6 us; the launch traced here: 44.5 us
  Pallas kernels  43.7 us (98%)
  local copies, waits for them, and re-layouts  0.8 us (2%)
    pallas_call x1, Pallas kernels, shards(): pl.pallas_call(functools.partial(kernel, n_ctx), out_shape=pltpu.VMEM((ro...  43.7 us

profile of v3, /device:TPU:1, one launch (start us, length us, event | category | flops | bytes accessed | tf_op | source)
XLA Modules:
  0.0 44.5 jit_solution(14408061025297934848)
XLA Ops:
  0.0 43.7 %shard_map.82 = bf16[128,2048]{1,0:T(8,128)(2,1)S(1)} custom-call(bf16[512,4096]{1,0:T(8,128)(2,1)} %hid.1, bf16[4096,512]{1,0:T(8,128)(2,1)} %wq.1, bf16[4096,128]{1,0:T(8,128)(2,1)} %wk.1, bf16[4096,128]{1,0:T(8,128)(2,1)} %wv.1, f32[1,128]{1,0:T(1,128)} %bitcast.2, f32[1,128]{1,0:T(1,128)} %bitcast.3, f32[1,128]{1,0:T(1,128)} %constant.2.clone.freq, ...), custom_call_target="tpu_custom_call" | custom-call | tf_op jit(solution)/shard_map/pallas_call | solution.py:333
  43.7 0.8 %copy.10 = bf16[128,2048]{1,0:T(8,128)(2,1)} copy(bf16[128,2048]{1,0:T(8,128)(2,1)S(1)} %shard_map.82) | data formatting | bytes 1048576

commit v4 on v3

--- a/solution.py
+++ b/solution.py
@@ -175,11 +175,11 @@
         if n == 0:
             pl.semaphore_wait(barrier, 5 + (x == 1).astype(jnp.int32) - (x == 3).astype(jnp.int32))
         for piece in pieces[4 * n : 4 * n + 4]:
-            near_copy(*piece).start()
-
             @pl.when(x < 3)
             def _():
                 second_copy(*piece).start()
+
+            near_copy(*piece).start()
 
     qsum = None
     for i, part in enumerate(parts):

time: 44.6 us -> 44.4 us (level)
  Pallas kernels: 43.7 us -> 43.1 us
    pallas_call x1, Pallas kernels: 43.7 us -> 43.1 us  [shards(): pl.pallas_call(functools.partial(kernel, n_ctx), out_shape=pltpu.VMEM((ro...]
where the time goes in v4:
time: 44.4 us; the launch traced here: 43.9 us
  Pallas kernels  43.1 us (97%)
  local copies, waits for them, and re-layouts  0.8 us (2%)
    pallas_call x1, Pallas kernels, shards(): pl.pallas_call(functools.partial(kernel, n_ctx), out_shape=pltpu.VMEM((ro...  43.1 us

profile of v4, /device:TPU:1, one launch (start us, length us, event | category | flops | bytes accessed | tf_op | source)
XLA Modules:
  0.0 43.9 jit_solution(6099247800326340978)
XLA Ops:
  0.0 43.1 %shard_map.82 = bf16[128,2048]{1,0:T(8,128)(2,1)S(1)} custom-call(bf16[512,4096]{1,0:T(8,128)(2,1)} %hid.1, bf16[4096,512]{1,0:T(8,128)(2,1)} %wq.1, bf16[4096,128]{1,0:T(8,128)(2,1)} %wk.1, bf16[4096,128]{1,0:T(8,128)(2,1)} %wv.1, f32[1,128]{1,0:T(1,128)} %bitcast.2, f32[1,128]{1,0:T(1,128)} %bitcast.3, f32[1,128]{1,0:T(1,128)} %constant.2.clone.freq, ...), custom_call_target="tpu_custom_call" | custom-call | tf_op jit(solution)/shard_map/pallas_call | solution.py:333
  43.1 0.8 %copy.10 = bf16[128,2048]{1,0:T(8,128)(2,1)} copy(bf16[128,2048]{1,0:T(8,128)(2,1)S(1)} %shard_map.82) | data formatting | bytes 1048576
